TPU v7x, 32 devices: a whole 2x2x4 slice. The times are simulated.
32 devices in a mesh: layer: 2 (over core), energy: 4 (over y, x), momentum: 4 (over z).
Axes of the slice: x: 2, y: 2, z: 4, core: 2. Of those that a mesh axis runs over, the one named last changes fastest.
Arguments:
- diag_blocks: float32 [4, 4, 4, 2, 384, 384], P('momentum', 'layer', 'energy'), may hold values from -1 to 5
- couplings: float32 [4, 4, 2, 384, 384], P('momentum', 'layer'), may hold values from -0.15625 to 0.15625
- phonon_matrix: float32 [4, 4], replicated, may hold values from -3 to 3
- mode_strength: float32 [3], replicated, may hold values from 0.5 to 2
- transfer_mode: int32 [4], replicated, may hold values from 0 to 2, as said below
- energy_offset: int32 [3], replicated, may hold values from 0 to 1, as said below
Outputs:
- self_energy: float32 [4, 2, 4, 2, 384, 384], P('momentum', 'layer', 'energy')
Inputs may be any that keep to these rules, and one draw needn't show every extreme that they name: `transfer_mode`: every one of the 3 modes is the mode of some transfer. `energy_offset`: some mode has offset 0 and some mode has offset 1.
All inputs are finite; a program needn't handle non-finite values.
Results may differ from a plain program's by a relative error of at most 0.00011.
Values sent between devices are 32-bit elements; how exact they have to be, the bound alone decides.
A program may use at most 64 MiB of HBM per device.

v0:
```python
from functools import partial

import jax
import jax.numpy as jnp
from jax import lax
from jax.experimental import pallas as pl
from jax.experimental.pallas import tpu as pltpu
from jax.sharding import PartitionSpec as P

MESH = pl.DeviceIdType.MESH
F32 = jnp.float32
BF16 = jnp.bfloat16
LANES = 128


def split(value):
    high = value.astype(BF16)
    low = (value - high.astype(F32)).astype(BF16)
    return high, low


def put_left(left, rows, n, value):
    columns = pl.ds(n * 2 * LANES, 2 * LANES)
    for ref, part in zip(left, split(value)):
        ref[rows, columns] = part


def put_right(right, c, n, value):
    for ref, part in zip(right, split(value)):
        base = c * 2 * LANES
        ref[n, base:base + LANES, :] = part
        ref[n, base + LANES:base + 2 * LANES, :LANES] = -part[:, LANES:]
        ref[n, base + LANES:base + 2 * LANES, LANES:] = part[:, :LANES]


def put_right_all(right, n, value):
    for c in range(value.shape[0] // LANES):
        put_right(right, c, n, value[c * LANES:(c + 1) * LANES])


def dot(a, b):
    return jnp.dot(a, b, preferred_element_type=F32)


def product(left, right, n):
    left_high, left_low = left[0][...], left[1][...]
    right_high, right_low = right[0][n], right[1][n]
    return dot(left_high, right_high) + dot(left_high, right_low) + dot(left_low, right_high)


def kernel(
    chunks, nodes, energies, momenta,
    diag, coup, phonon, strength, transfer, offset, out,
    diag_odd, diag_even, c_even, c_odd, c_odd_left,
    x_own, x_left, lo_send, lo_recv, up_own, up_left, low_own, low_left,
    lt_send, lt_recv, ut_send, ut_recv, reduced, gbuf, rbuf, tbuf, obuf, kern,
    la_h, la_l, lb_h, lb_l, lc_h, lc_l,
    ra_h, ra_l, rb_h, rb_l, rc_h, rc_l,
    in_sem, l_send, l_recv, f_send, f_recv, b_send, b_recv,
):
    la, lb, lc = (la_h, la_l), (lb_h, lb_l), (lc_h, lc_l)
    ra, rb, rc = (ra_h, ra_l), (rb_h, rb_l), (rc_h, rc_l)
    order = chunks * LANES
    me = lax.axis_index("layer")
    here_k = lax.axis_index("momentum")
    here_e = lax.axis_index("energy")
    peers = energies * momenta
    here = here_k * energies + here_e
    rows = order // peers
    has_right = me < nodes - 1
    has_left = me > 0

    loads = []
    for s, (src, dst) in enumerate(
        ((diag.at[1], diag_odd), (coup.at[0], c_even), (coup.at[1], c_odd), (diag.at[0], diag_even))
    ):
        load = pltpu.make_async_copy(src, dst, in_sem.at[s])
        load.start()
        loads.append(load)

    barrier = pltpu.get_barrier_semaphore()

    @pl.when(has_right)
    def _():
        pl.semaphore_signal(barrier, inc=1, device_id={"layer": me + 1}, device_id_type=MESH)

    @pl.when(has_left)
    def _():
        pl.semaphore_signal(barrier, inc=1, device_id={"layer": me - 1}, device_id_type=MESH)

    def greet(d, carry):
        peer = lax.rem(here + d, peers)
        pl.semaphore_signal(
            barrier, inc=1,
            device_id={"momentum": peer // energies, "energy": lax.rem(peer, energies)},
            device_id_type=MESH,
        )
        return carry

    lax.fori_loop(1, peers, greet, 0)

    def to_layer(slot, src, dst, step):
        return pltpu.make_async_remote_copy(
            src_ref=src, dst_ref=dst, send_sem=l_send.at[slot], recv_sem=l_recv.at[slot],
            device_id={"layer": me + step}, device_id_type=MESH,
        )

    send_c = to_layer(0, c_odd, c_odd_left, 1)
    send_x = to_layer(1, x_own, x_left, 1)
    send_lo = to_layer(2, lo_send, lo_recv, -1)
    send_up = to_layer(3, up_own, up_left, 1)
    send_low = to_layer(4, low_own, low_left, 1)
    send_lt = to_layer(5, lt_send, lt_recv, 1)
    send_ut = to_layer(6, ut_send, ut_recv, -1)

    eye = (
        lax.broadcasted_iota(jnp.int32, (LANES, LANES), 0)
        == lax.broadcasted_iota(jnp.int32, (LANES, LANES), 1)
    )
    two = jnp.where(eye, F32(2.0), F32(0.0))

    def prepare_inverse(read):
        row_inv, col_inv = [], []
        for c in range(chunks):
            block = read(c, c)
            real = jnp.where(eye, block[:, :LANES], 0.0)
            imag = jnp.where(eye, block[:, LANES:], 0.0)
            for axis, found in ((0, row_inv), (1, col_inv)):
                r = jnp.sum(real, axis=axis, keepdims=True)
                i = jnp.sum(imag, axis=axis, keepdims=True)
                modulus = r * r + i * i
                found.append((r / modulus, -i / modulus))
        for n in range(chunks):
            for c in range(chunks):
                block = read(c, n)
                put_left(la, slice(c * LANES, (c + 1) * LANES), n, block)
                a_r, a_i = block[:, :LANES], block[:, LANES:]
                x_r, x_i = row_inv[n]
                y_r, y_i = col_inv[c]
                res_r = a_i * x_i - a_r * x_r
                if c == n:
                    res_r = res_r + two
                res_i = -(a_r * x_i + a_i * x_r)
                first = jnp.concatenate(
                    [y_r * res_r - y_i * res_i, y_r * res_i + y_i * res_r], axis=1
                )
                put_left(lb, slice(c * LANES, (c + 1) * LANES), n, first)
                put_right(ra, c, n, first)

    def residual(n):
        acc = product(la, ra, n)
        for c in range(chunks):
            same = jnp.where(n == c, F32(1.0), F32(0.0))
            block = acc[c * LANES:(c + 1) * LANES]
            block = jnp.concatenate([two * same - block[:, :LANES], -block[:, LANES:]], axis=1)
            put_right(rb, c, n, block)

    def each(fn):
        lax.fori_loop(0, chunks, lambda n, carry: (fn(n), carry)[1], 0)

    def pair_block(ref, c, n):
        rs, cs = slice(c * LANES, (c + 1) * LANES), slice(n * LANES, (n + 1) * LANES)
        return jnp.concatenate([ref[0, rs, cs], ref[1, rs, cs]], axis=1)

    def adjoint_block(ref, c, n):
        rs, cs = slice(n * LANES, (n + 1) * LANES), slice(c * LANES, (c + 1) * LANES)
        return jnp.concatenate([ref[0, rs, cs].T, -ref[1, rs, cs].T], axis=1)

    every = slice(0, order)

    loads[0].wait()
    prepare_inverse(lambda c, n: pair_block(diag_odd, c, n))
    each(residual)

    neighbours = jnp.where(has_left, 1, 0) + jnp.where(has_right, 1, 0)
    pl.semaphore_wait(barrier, peers - 1 + neighbours)
    loads[2].wait()

    @pl.when(has_right)
    def _():
        send_c.start()

    def odd_inverse(n):
        acc = product(lb, rb, n)
        x_own[n] = acc
        put_right_all(ra, n, acc)

    each(odd_inverse)

    @pl.when(has_right)
    def _():
        send_x.start()

    loads[1].wait()
    for n in range(chunks):
        for c in range(chunks):
            put_left(la, slice(c * LANES, (c + 1) * LANES), n, pair_block(c_even, c, n))
            put_right(rb, c, n, adjoint_block(c_even, c, n))

    each(lambda n: put_left(lb, every, n, product(la, ra, n)))

    @pl.when(has_left)
    def _():
        send_c.wait_recv()
        for n in range(chunks):
            for c in range(chunks):
                put_left(la, slice(c * LANES, (c + 1) * LANES), n, adjoint_block(c_odd_left, c, n))
                put_right(rc, c, n, pair_block(c_odd_left, c, n))
        send_x.wait_recv()

        def embed(n):
            put_right_all(ra, n, x_left[n])

        each(embed)

        def left_odd(n):
            acc = product(la, ra, n)
            lo_send[n] = acc
            put_left(lc, every, n, acc)

        each(left_odd)
        send_lo.start()

    loads[3].wait()
    for n in range(chunks):
        for c in range(chunks):
            reduced[n, c * LANES:(c + 1) * LANES, :] = pair_block(diag_even, c, n)

    def subtract_own(n):
        reduced[n] = reduced[n] - product(lb, rb, n)

    each(subtract_own)

    @pl.when(has_left)
    def _():
        def subtract_edge(n):
            reduced[n] = reduced[n] - product(lc, rc, n)

        each(subtract_edge)

    @pl.when(has_right)
    def _():
        for n in range(chunks):
            for c in range(chunks):
                put_right(rc, c, n, pair_block(c_odd, c, n))

        def upper(n):
            up_own[n] = product(lb, rc, n)

        each(upper)
        send_up.start()
        send_lo.wait_recv()

        def embed(n):
            put_left(lc, every, n, lo_recv[n])

        each(embed)

        def lower(n):
            low_own[n] = product(lc, rb, n)

        each(lower)
        send_low.start()

    prepare_inverse(lambda c, n: reduced[n, c * LANES:(c + 1) * LANES, :])
    each(residual)
    each(lambda n: put_right_all(ra, n, product(lb, rb, n)))

    @pl.when(has_right)
    def _():
        def embed(n):
            put_left(la, every, n, low_own[n])
            put_right_all(rb, n, up_own[n])

        each(embed)
        each(lambda n: put_left(lb, every, n, product(la, ra, n)))

        def lower_term(n):
            lt_send[n] = product(lb, rb, n)

        each(lower_term)
        send_lt.start()

    @pl.when(has_left)
    def _():
        send_up.wait_recv()
        send_low.wait_recv()

        def embed(n):
            put_left(la, every, n, up_left[n])
            put_right_all(rb, n, low_left[n])

        each(embed)
        each(lambda n: put_left(lb, every, n, product(la, ra, n)))

        def upper_term(n):
            ut_send[n] = product(lb, rb, n)

        each(upper_term)
        send_ut.start()

    @pl.when(has_left)
    def _():
        send_lt.wait_recv()

        def take(n):
            reduced[n] = reduced[n] - lt_recv[n]

        each(take)

    @pl.when(has_right)
    def _():
        send_ut.wait_recv()

        def take(n):
            reduced[n] = reduced[n] - ut_recv[n]

        each(take)

    prepare_inverse(lambda c, n: reduced[n, c * LANES:(c + 1) * LANES, :])

    def forward(n, peer, at):
        return pltpu.make_async_remote_copy(
            src_ref=gbuf.at[n, pl.ds(peer * rows, rows), :],
            dst_ref=rbuf.at[n, at],
            send_sem=f_send.at[n, peer],
            recv_sem=f_recv.at[n, at],
            device_id={"momentum": peer // energies, "energy": lax.rem(peer, energies)},
            device_id_type=MESH,
        )

    def backward(n, peer, at):
        return pltpu.make_async_remote_copy(
            src_ref=tbuf.at[n, peer],
            dst_ref=obuf.at[n, pl.ds(at * rows, rows), :],
            send_sem=b_send.at[n, peer],
            recv_sem=b_recv.at[n, at],
            device_id={"momentum": peer // energies, "energy": lax.rem(peer, energies)},
            device_id_type=MESH,
        )

    def around(fn):
        def step(d, carry):
            fn(lax.rem(here + d, peers))
            return carry

        lax.fori_loop(1, peers, step, 0)

    def finish(n):
        residual(n)
        gbuf[n] = product(lb, rb, n)
        around(lambda peer: forward(n, peer, here).start())
        rbuf[n, here] = gbuf[n, pl.ds(pl.multiple_of(here * rows, 8), rows), :]

    each(finish)

    transfers = transfer.shape[0]
    for q in range(transfers):
        mode = transfer[q]
        gain = strength[mode]
        moved = offset[mode]
        for e in range(energies):
            for f in range(energies):
                total = F32(0.0)
                for s in range(energies):
                    hits = jnp.where(s == e - moved, F32(1.0), F32(0.0)) + jnp.where(
                        s == e + moved, F32(1.0), F32(0.0)
                    )
                    total = total + hits * phonon[s, f]
                kern[(q * energies + e) * energies + f] = gain * total

    def combine(n):
        around(lambda peer: forward(n, here, peer).wait_recv())
        for k in range(momenta):
            for e in range(energies):
                total = None
                for source in range(momenta):
                    q = (k - source) % transfers
                    for f in range(energies):
                        term = kern[(q * energies + e) * energies + f] * rbuf[n, source * energies + f]
                        total = term if total is None else total + term
                tbuf[n, k * energies + e] = total
        around(lambda peer: backward(n, peer, here).start())
        obuf[n, pl.ds(pl.multiple_of(here * rows, 8), rows), :] = tbuf[n, here]

    each(combine)

    for n in range(chunks):
        around(lambda peer: backward(n, here, peer).wait_recv())
        columns = slice(n * LANES, (n + 1) * LANES)
        out[0, :, columns] = obuf[n, :, :LANES]
        out[1, :, columns] = obuf[n, :, LANES:]

    def drain(n):
        around(lambda peer: forward(n, peer, here).wait_send())
        around(lambda peer: backward(n, peer, here).wait_send())

    each(drain)

    @pl.when(has_right)
    def _():
        for copy in (send_c, send_x, send_up, send_low, send_lt):
            copy.wait_send()

    @pl.when(has_left)
    def _():
        for copy in (send_lo, send_ut):
            copy.wait_send()


def body(diag_blocks, couplings, phonon_matrix, mode_strength, transfer_mode, energy_offset):
    order = diag_blocks.shape[-1]
    chunks = order // LANES
    nodes = lax.axis_size("layer")
    energies = lax.axis_size("energy")
    momenta = lax.axis_size("momentum")
    peers = energies * momenta
    diag = diag_blocks.reshape(2, 2, order, order)
    coup = couplings.reshape(2, 2, order, order)
    plain = pltpu.VMEM((2, order, order), F32)
    chunked = pltpu.VMEM((chunks, order, 2 * LANES), F32)
    pieces = pltpu.VMEM((chunks, peers, order // peers, 2 * LANES), F32)
    left = pltpu.VMEM((order, 2 * order), BF16)
    right = pltpu.VMEM((chunks, 2 * order, 2 * LANES), BF16)
    smem = pl.BlockSpec(memory_space=pltpu.SMEM)
    anywhere = pl.BlockSpec(memory_space=pl.ANY)
    transfers = transfer_mode.shape[0]
    dma = pltpu.SemaphoreType.DMA
    result = pl.pallas_call(
        partial(kernel, chunks, nodes, energies, momenta),
        out_shape=jax.ShapeDtypeStruct((2, order, order), F32),
        in_specs=[anywhere, anywhere, smem, smem, smem, smem],
        out_specs=pl.BlockSpec(memory_space=pltpu.VMEM),
        scratch_shapes=[plain] * 5 + [chunked] * 13 + [chunked, pieces, pieces, chunked]
        + [pltpu.SMEM((transfers * energies * energies,), F32)]
        + [left] * 6 + [right] * 6
        + [dma((4,)), dma((7,)), dma((7,))] + [dma((chunks, peers))] * 4,
        compiler_params=pltpu.CompilerParams(
            collective_id=0, has_side_effects=True, vmem_limit_bytes=60 * 1024 * 1024
        ),
    )(diag, coup, phonon_matrix, mode_strength, transfer_mode, energy_offset)
    return result[None, None, None]


def solution(mesh):
    return jax.shard_map(
        body,
        mesh=mesh,
        in_specs=(
            P("momentum", "layer", "energy", None, None, None),
            P("momentum", "layer", None, None, None),
            P(),
            P(),
            P(),
            P(),
        ),
        out_specs=P("momentum", "layer", "energy", None, None, None),
        check_vma=False,
    )
```

profile of v0, /device:TPU:9, one launch (start us, length us, event | category | flops | bytes accessed | tf_op | source)
XLA Modules:
  0.0 90.9 jit_solution(3528944874881214391)
XLA Ops:
  0.0 88.5 %shard_map.64 = f32[2,384,384]{2,1,0:T(8,128)} custom-call(f32[2,2,384,384]{3,2,1,0:T(8,128)} %bitcast.4, f32[2,2,384,384]{3,2,1,0:T(8,128)} %bitcast.5, f32[4,4]{1,0:T(4,128)} %phonon.1, f32[3]{0:T(128)} %strength.1, s32[4]{0:T(128)} %transfer.1, s32[3]{0:T(128)} %offset.1), custom_call_target="tpu_custom_call" | custom-call | tf_op jit(solution)/shard_map/pallas_call | solution.py:429
  88.5 2.4 %copy.8 = f32[1,1,1,2,384,384]{5,4,3,2,1,0:T(8,128)} copy(f32[1,1,1,2,384,384]{5,4,3,2,1,0:T(8,128)} %bitcast.3) | data formatting | bytes 2359296
where the time goes:
time: 91 us; the launch traced here: 90.9 us
  Pallas kernels  88.5 us (97%)
  local copies, waits for them, and re-layouts  2.36 us (3%)
    pallas_call x1, Pallas kernels, body(): pl.pallas_call(partial(kernel, chunks, nodes, energies, momenta), out_sha...  88.5 us
    unnamed x1, local copies, waits for them, and re-layouts  2.36 us

commit v1 on v0

--- a/solution.py
+++ b/solution.py
@@ -43,9 +43,14 @@
 
 
 def product(left, right, n):
-    left_high, left_low = left[0][...], left[1][...]
     right_high, right_low = right[0][n], right[1][n]
-    return dot(left_high, right_high) + dot(left_high, right_low) + dot(left_low, right_high)
+    parts = []
+    for m in range(0, left[0].shape[0], LANES):
+        left_high, left_low = left[0][m:m + LANES, :], left[1][m:m + LANES, :]
+        parts.append(
+            dot(left_high, right_high) + dot(left_high, right_low) + dot(left_low, right_high)
+        )
+    return jnp.concatenate(parts, axis=0)
 
 
 def kernel(
@@ -100,8 +105,9 @@
     lax.fori_loop(1, peers, greet, 0)
 
     def to_layer(slot, src, dst, step):
-        return pltpu.make_async_remote_copy(
-            src_ref=src, dst_ref=dst, send_sem=l_send.at[slot], recv_sem=l_recv.at[slot],
+        return lambda n: pltpu.make_async_remote_copy(
+            src_ref=src.at[n], dst_ref=dst.at[n],
+            send_sem=l_send.at[slot, n], recv_sem=l_recv.at[slot, n],
             device_id={"layer": me + step}, device_id_type=MESH,
         )
 
@@ -150,12 +156,16 @@
     def residual(n):
         acc = product(la, ra, n)
         for c in range(chunks):
-            same = jnp.where(n == c, F32(1.0), F32(0.0))
-            block = acc[c * LANES:(c + 1) * LANES]
-            block = jnp.concatenate([two * same - block[:, :LANES], -block[:, LANES:]], axis=1)
+            block = -acc[c * LANES:(c + 1) * LANES]
+            if c == n:
+                block = jnp.concatenate([two + block[:, :LANES], block[:, LANES:]], axis=1)
             put_right(rb, c, n, block)
 
     def each(fn):
+        for n in range(chunks):
+            fn(n)
+
+    def loop(fn):
         lax.fori_loop(0, chunks, lambda n, carry: (fn(n), carry)[1], 0)
 
     def pair_block(ref, c, n):
@@ -178,18 +188,20 @@
 
     @pl.when(has_right)
     def _():
-        send_c.start()
+        send_c(0).start()
+        send_c(1).start()
 
     def odd_inverse(n):
         acc = product(lb, rb, n)
         x_own[n] = acc
+
+        @pl.when(has_right)
+        def _():
+            send_x(n).start()
+
         put_right_all(ra, n, acc)
 
     each(odd_inverse)
-
-    @pl.when(has_right)
-    def _():
-        send_x.start()
 
     loads[1].wait()
     for n in range(chunks):
@@ -201,14 +213,15 @@
 
     @pl.when(has_left)
     def _():
-        send_c.wait_recv()
+        send_c(0).wait_recv()
+        send_c(1).wait_recv()
         for n in range(chunks):
             for c in range(chunks):
                 put_left(la, slice(c * LANES, (c + 1) * LANES), n, adjoint_block(c_odd_left, c, n))
                 put_right(rc, c, n, pair_block(c_odd_left, c, n))
-        send_x.wait_recv()
 
         def embed(n):
+            send_x(n).wait_recv()
             put_right_all(ra, n, x_left[n])
 
         each(embed)
@@ -216,10 +229,10 @@
         def left_odd(n):
             acc = product(la, ra, n)
             lo_send[n] = acc
+            send_lo(n).start()
             put_left(lc, every, n, acc)
 
         each(left_odd)
-        send_lo.start()
 
     loads[3].wait()
     for n in range(chunks):
@@ -246,21 +259,21 @@
 
         def upper(n):
             up_own[n] = product(lb, rc, n)
+            send_up(n).start()
 
         each(upper)
-        send_up.start()
-        send_lo.wait_recv()
 
         def embed(n):
+            send_lo(n).wait_recv()
             put_left(lc, every, n, lo_recv[n])
 
         each(embed)
 
         def lower(n):
             low_own[n] = product(lc, rb, n)
+            send_low(n).start()
 
         each(lower)
-        send_low.start()
 
     prepare_inverse(lambda c, n: reduced[n, c * LANES:(c + 1) * LANES, :])
     each(residual)
@@ -277,16 +290,16 @@
 
         def lower_term(n):
             lt_send[n] = product(lb, rb, n)
+            send_lt(n).start()
 
         each(lower_term)
-        send_lt.start()
-
-    @pl.when(has_left)
-    def _():
-        send_up.wait_recv()
-        send_low.wait_recv()
+
+    @pl.when(has_left)
+    def _():
 
         def embed(n):
+            send_up(n).wait_recv()
+            send_low(n).wait_recv()
             put_left(la, every, n, up_left[n])
             put_right_all(rb, n, low_left[n])
 
@@ -295,24 +308,24 @@
 
         def upper_term(n):
             ut_send[n] = product(lb, rb, n)
+            send_ut(n).start()
 
         each(upper_term)
-        send_ut.start()
-
-    @pl.when(has_left)
-    def _():
-        send_lt.wait_recv()
+
+    @pl.when(has_left)
+    def _():
 
         def take(n):
+            send_lt(n).wait_recv()
             reduced[n] = reduced[n] - lt_recv[n]
 
         each(take)
 
     @pl.when(has_right)
     def _():
-        send_ut.wait_recv()
 
         def take(n):
+            send_ut(n).wait_recv()
             reduced[n] = reduced[n] - ut_recv[n]
 
         each(take)
@@ -383,7 +396,7 @@
         around(lambda peer: backward(n, peer, here).start())
         obuf[n, pl.ds(pl.multiple_of(here * rows, 8), rows), :] = tbuf[n, here]
 
-    each(combine)
+    loop(combine)
 
     for n in range(chunks):
         around(lambda peer: backward(n, here, peer).wait_recv())
@@ -395,17 +408,19 @@
         around(lambda peer: forward(n, peer, here).wait_send())
         around(lambda peer: backward(n, peer, here).wait_send())
 
-    each(drain)
-
-    @pl.when(has_right)
-    def _():
-        for copy in (send_c, send_x, send_up, send_low, send_lt):
-            copy.wait_send()
-
-    @pl.when(has_left)
-    def _():
-        for copy in (send_lo, send_ut):
-            copy.wait_send()
+    loop(drain)
+
+    @pl.when(has_right)
+    def _():
+        for n in range(2):
+            send_c(n).wait_send()
+        for send in (send_x, send_up, send_low, send_lt):
+            each(lambda n: send(n).wait_send())
+
+    @pl.when(has_left)
+    def _():
+        for send in (send_lo, send_ut):
+            each(lambda n: send(n).wait_send())
 
 
 def body(diag_blocks, couplings, phonon_matrix, mode_strength, transfer_mode, energy_offset):
@@ -434,7 +449,7 @@
         scratch_shapes=[plain] * 5 + [chunked] * 13 + [chunked, pieces, pieces, chunked]
         + [pltpu.SMEM((transfers * energies * energies,), F32)]
         + [left] * 6 + [right] * 6
-        + [dma((4,)), dma((7,)), dma((7,))] + [dma((chunks, peers))] * 4,
+        + [dma((4,))] + [dma((7, max(2, chunks)))] * 2 + [dma((chunks, peers))] * 4,
         compiler_params=pltpu.CompilerParams(
             collective_id=0, has_side_effects=True, vmem_limit_bytes=60 * 1024 * 1024
         ),

time: 91 us -> 87.3 us (0.959)
  Pallas kernels: 88.5 us -> 84.5 us
    pallas_call x1, Pallas kernels: 88.5 us -> 84.5 us  [body(): pl.pallas_call(partial(kernel, chunks, nodes, energies, momenta), out_sha...]
where the time goes in v1:
time: 87.3 us; the launch traced here: 86.9 us
  Pallas kernels  84.5 us (97%)
  local copies, waits for them, and re-layouts  2.36 us (3%)
    pallas_call x1, Pallas kernels, body(): pl.pallas_call(partial(kernel, chunks, nodes, energies, momenta), out_sha...  84.5 us
    unnamed x1, local copies, waits for them, and re-layouts  2.36 us

profile of v1, /device:TPU:9, one launch (start us, length us, event | category | flops | bytes accessed | tf_op | source)
XLA Modules:
  0.0 86.9 jit_solution(5287938432013806394)
XLA Ops:
  0.0 84.5 %shard_map.64 = f32[2,384,384]{2,1,0:T(8,128)} custom-call(f32[2,2,384,384]{3,2,1,0:T(8,128)} %bitcast.4, f32[2,2,384,384]{3,2,1,0:T(8,128)} %bitcast.5, f32[4,4]{1,0:T(4,128)} %phonon.1, f32[3]{0:T(128)} %strength.1, s32[4]{0:T(128)} %transfer.1, s32[3]{0:T(128)} %offset.1), custom_call_target="tpu_custom_call" | custom-call | tf_op jit(solution)/shard_map/pallas_call | solution.py:444
  84.5 2.4 %copy.8 = f32[1,1,1,2,384,384]{5,4,3,2,1,0:T(8,128)} copy(f32[1,1,1,2,384,384]{5,4,3,2,1,0:T(8,128)} %bitcast.3) | data formatting | bytes 2359296

commit v2 on v1

--- a/solution.py
+++ b/solution.py
@@ -182,23 +182,9 @@
     prepare_inverse(lambda c, n: pair_block(diag_odd, c, n))
     each(residual)
 
-    neighbours = jnp.where(has_left, 1, 0) + jnp.where(has_right, 1, 0)
-    pl.semaphore_wait(barrier, peers - 1 + neighbours)
-    loads[2].wait()
-
-    @pl.when(has_right)
-    def _():
-        send_c(0).start()
-        send_c(1).start()
-
     def odd_inverse(n):
         acc = product(lb, rb, n)
         x_own[n] = acc
-
-        @pl.when(has_right)
-        def _():
-            send_x(n).start()
-
         put_right_all(ra, n, acc)
 
     each(odd_inverse)
@@ -210,6 +196,26 @@
             put_right(rb, c, n, adjoint_block(c_even, c, n))
 
     each(lambda n: put_left(lb, every, n, product(la, ra, n)))
+
+    neighbours = jnp.where(has_left, 1, 0) + jnp.where(has_right, 1, 0)
+    pl.semaphore_wait(barrier, peers - 1 + neighbours)
+    loads[2].wait()
+
+    @pl.when(has_right)
+    def _():
+        send_c(0).start()
+        send_c(1).start()
+        each(lambda n: send_x(n).start())
+
+    loads[3].wait()
+    for n in range(chunks):
+        for c in range(chunks):
+            reduced[n, c * LANES:(c + 1) * LANES, :] = pair_block(diag_even, c, n)
+
+    def subtract_own(n):
+        reduced[n] = reduced[n] - product(lb, rb, n)
+
+    each(subtract_own)
 
     @pl.when(has_left)
     def _():
@@ -233,16 +239,6 @@
             put_left(lc, every, n, acc)
 
         each(left_odd)
-
-    loads[3].wait()
-    for n in range(chunks):
-        for c in range(chunks):
-            reduced[n, c * LANES:(c + 1) * LANES, :] = pair_block(diag_even, c, n)
-
-    def subtract_own(n):
-        reduced[n] = reduced[n] - product(lb, rb, n)
-
-    each(subtract_own)
 
     @pl.when(has_left)
     def _():

time: 87.3 us -> 89.6 us (1.026)
  Pallas kernels: 84.5 us -> 87.1 us
    pallas_call x1, Pallas kernels: 84.5 us -> 87.1 us  [body(): pl.pallas_call(partial(kernel, chunks, nodes, energies, momenta), out_sha...]
where the time goes in v2:
time: 89.6 us; the launch traced here: 89.5 us
  Pallas kernels  87.1 us (97%)
  local copies, waits for them, and re-layouts  2.36 us (3%)
    pallas_call x1, Pallas kernels, body(): pl.pallas_call(partial(kernel, chunks, nodes, energies, momenta), out_sha...  87.1 us
    unnamed x1, local copies, waits for them, and re-layouts  2.36 us

profile of v2, /device:TPU:9, one launch (start us, length us, event | category | flops | bytes accessed | tf_op | source)
XLA Modules:
  0.0 89.5 jit_solution(13098539354286259212)
XLA Ops:
  0.0 87.1 %shard_map.64 = f32[2,384,384]{2,1,0:T(8,128)} custom-call(f32[2,2,384,384]{3,2,1,0:T(8,128)} %bitcast.4, f32[2,2,384,384]{3,2,1,0:T(8,128)} %bitcast.5, f32[4,4]{1,0:T(4,128)} %phonon.1, f32[3]{0:T(128)} %strength.1, s32[4]{0:T(128)} %transfer.1, s32[3]{0:T(128)} %offset.1), custom_call_target="tpu_custom_call" | custom-call | tf_op jit(solution)/shard_map/pallas_call | solution.py:440
  87.1 2.4 %copy.8 = f32[1,1,1,2,384,384]{5,4,3,2,1,0:T(8,128)} copy(f32[1,1,1,2,384,384]{5,4,3,2,1,0:T(8,128)} %bitcast.3) | data formatting | bytes 2359296
